TPU v7x, 32 devices: a whole 2x2x4 slice. The times are simulated.
32 devices in a mesh: seq: 8 (over z, y), ctx: 4 (over x, core).
Axes of the slice: x: 2, y: 2, z: 4, core: 2. Of those that a mesh axis runs over, the one named last changes fastest.
Arguments:
- hidden_in: bfloat16 [8, 512, 1024], P('seq', 'ctx'), may hold values from -6 to 6
- positions: int32 [8, 512], P('seq', 'ctx'), may hold values from 0 to 499, as said below
- norm1_gain: float32 [1024], replicated, may hold values from 0.5 to 1.5
- w_query: bfloat16 [1024, 2048], P(('seq', 'ctx')), may hold values from -0.1875 to 0.1875
- key_weight_matrix: bfloat16 [1024, 1024], P(('seq', 'ctx')), may hold values from -0.1875 to 0.1875
- value_weight_matrix: bfloat16 [1024, 1024], P(('seq', 'ctx')), may hold values from -0.1875 to 0.1875
- query_gain: float32 [128], replicated, may hold values from 0.8 to 6
- key_gain: float32 [128], replicated, may hold values from 0.8 to 6
- w_out: bfloat16 [1024, 2048], P(('seq', 'ctx')), may hold values from -0.75 to 0.75
- norm2_gain: float32 [1024], replicated, may hold values from 0.5 to 1.5
- w_gate: bfloat16 [1024, 3072], P(('seq', 'ctx')), may hold values from -0.1875 to 0.1875
- w_up: bfloat16 [1024, 3072], P(('seq', 'ctx')), may hold values from -0.1875 to 0.1875
- w_down: bfloat16 [1024, 3072], P(('seq', 'ctx')), may hold values from -0.109375 to 0.109375
- cotangent: bfloat16 [8, 512, 1024], P('seq', 'ctx'), may hold values from -6 to 6
Outputs:
- out_hidden: bfloat16 [8, 512, 1024], P('seq', 'ctx')
- grad_hidden: bfloat16 [8, 512, 1024], P('seq', 'ctx')
- grad_query: float32 [1024, 2048], P(('seq', 'ctx'))
- grad_key: float32 [1024, 1024], P(('seq', 'ctx'))
- grad_value: float32 [1024, 1024], P(('seq', 'ctx'))
- grad_out: float32 [1024, 2048], P(('seq', 'ctx'))
- grad_gate: float32 [1024, 3072], P(('seq', 'ctx'))
- grad_up: float32 [1024, 3072], P(('seq', 'ctx'))
- grad_down: float32 [1024, 3072], P(('seq', 'ctx'))
- grad_norm1: float32 [1024], replicated
- grad_norm2: float32 [1024], replicated
- grad_query_gain: float32 [128], replicated
- grad_key_gain: float32 [128], replicated
Inputs may be any that keep to these rules, and one draw needn't show every extreme that they name: In each sequence positions are 0 at the first token and rise by one from token to token, except at the first token of a document, where they return to 0.
All inputs are finite; a program needn't handle non-finite values.
Results may differ from a plain program's by a relative error of at most 0.04.
The roundings to bfloat16 on the way count: a program that leaves them out, or rounds other values in their place, can miss the bound.
Values may be sent and summed in bfloat16 or wider, within the bound.
No kernel may reach another device: no remote copies, remote signals or barrier semaphores. Data moves between devices by JAX's collectives and lax.ppermute only.
A program may use at most 384 MiB of HBM per device.

v0:
```python
import jax
import jax.numpy as jnp
from jax import lax
from jax.sharding import PartitionSpec as P

NORM_EPSILON = 1e-06
ROPE_THETA = 1000000.0


def rope_tables(position_ids, head_width):
    half_width = head_width // 2
    inverse = ROPE_THETA ** (-(2.0 / head_width) * jnp.arange(half_width, dtype=jnp.float32))
    angles = position_ids.astype(jnp.float32)[:, None] * inverse[None, :]
    return (jnp.cos(angles), jnp.sin(angles))


def rotate(vectors, cosine, sine):
    half_width = vectors.shape[-1] // 2
    first = vectors[..., :half_width]
    second = vectors[..., half_width:]
    cos_rows = cosine[:, None, :]
    sin_rows = sine[:, None, :]
    return jnp.concatenate(
        (first * cos_rows - second * sin_rows, second * cos_rows + first * sin_rows), -1
    )


def rotate_back(grads, cosine, sine):
    half_width = grads.shape[-1] // 2
    first = grads[..., :half_width]
    second = grads[..., half_width:]
    cos_rows = cosine[:, None, :]
    sin_rows = sine[:, None, :]
    return jnp.concatenate(
        (first * cos_rows + second * sin_rows, second * cos_rows - first * sin_rows), -1
    )


def unit_rows(vectors):
    factor = lax.rsqrt(jnp.mean(vectors * vectors, -1, keepdims=True) + NORM_EPSILON)
    return (factor, vectors * factor)


def unit_back(grad_unit, factor, unit):
    return factor * (grad_unit - unit * jnp.mean(grad_unit * unit, -1, keepdims=True))


def outer_rows(left, right):
    return jnp.einsum("tj,tc->jc", left, right, preferred_element_type=jnp.float32)


def shards(
    hidden_in,
    positions,
    norm1_gain,
    w_query,
    key_weight_matrix,
    value_weight_matrix,
    query_gain,
    key_gain,
    w_out,
    norm2_gain,
    w_gate,
    w_up,
    w_down,
    cotangent,
):
    row_count = hidden_in.shape[1]
    head_width = query_gain.shape[0]
    query_columns = w_query.shape[1]
    key_value_columns = key_weight_matrix.shape[1]
    kv_heads = key_value_columns // head_width
    query_group_count = query_columns // key_value_columns
    attn_width = query_columns + 2 * key_value_columns + query_columns
    inputs = hidden_in[0].astype(jnp.float32)
    position_ids = positions[0]
    factor1, unit1 = unit_rows(inputs)
    normed1 = (unit1 * norm1_gain).astype(jnp.bfloat16)
    w_joint = jnp.concatenate((w_query, key_weight_matrix, value_weight_matrix), 1)
    joint_full, out_full = (
        lax.all_gather(w_joint, ("seq", "ctx"), axis=0, tiled=True),
        lax.all_gather(w_out, ("seq", "ctx"), axis=0, tiled=True),
    )
    projected_output = jnp.dot(normed1, joint_full, preferred_element_type=jnp.float32)
    query_raw = projected_output[:, :query_columns].reshape(
        row_count, query_columns // head_width, head_width
    )
    unrotated_key = projected_output[:, query_columns : query_columns + key_value_columns].reshape(
        row_count, kv_heads, head_width
    )
    unprojected_value = projected_output[:, query_columns + key_value_columns :].reshape(
        row_count, kv_heads, head_width
    )
    query_factor, query_unit = unit_rows(query_raw)
    key_factor, key_unit = unit_rows(unrotated_key)
    cosine, sine = rope_tables(position_ids, head_width)
    rotated_query = rotate(query_unit * query_gain, cosine, sine).astype(jnp.bfloat16)
    key_rot = rotate(key_unit * key_gain, cosine, sine).astype(jnp.bfloat16)
    query_head_rows = rotated_query.reshape(
        row_count, kv_heads, query_group_count, head_width
    ).transpose(1, 2, 0, 3)
    own_pair = jnp.stack((key_rot, unprojected_value.astype(jnp.bfloat16)))
    cycle_size = lax.axis_size("ctx")
    my_block = lax.axis_index("ctx")
    offsets = jnp.arange(row_count, dtype=jnp.int32)
    query_index = my_block * row_count + offsets
    doc_begin = query_index - position_ids
    score_scale = head_width ** (-0.5)

    def visible(count):
        key_index = jnp.arange(count, dtype=jnp.int32)
        return (key_index[None, :] <= query_index[:, None]) & (
            key_index[None, :] >= doc_begin[:, None]
        )

    def block_scores(key_value_couple, key_mask):
        scores = score_scale * jnp.einsum(
            "ekla,xea->eklx",
            query_head_rows,
            key_value_couple[0],
            preferred_element_type=jnp.float32,
        )
        return jnp.where(key_mask[None, None], scores, -jnp.inf)

    state = (
        jnp.full((kv_heads, query_group_count, row_count), -jnp.inf, jnp.float32),
        jnp.zeros((kv_heads, query_group_count, row_count), jnp.float32),
        jnp.zeros((kv_heads, query_group_count, row_count, head_width), jnp.float32),
    )
    key_value_couple = lax.all_gather(own_pair, "ctx", axis=1, tiled=True)
    key_mask = visible(key_value_couple.shape[1])

    def attend(current):
        highest, totals, accum = current
        scores = block_scores(key_value_couple, key_mask)
        new_high = jnp.max(scores, -1)
        decay = jnp.exp(highest - new_high)
        weights = jnp.exp(scores - new_high[..., None])
        totals = totals * decay + jnp.sum(weights, -1)
        accum = accum * decay[..., None] + jnp.einsum(
            "emaj,jep->emap",
            weights.astype(jnp.bfloat16),
            key_value_couple[1],
            preferred_element_type=jnp.float32,
        )
        return (new_high, totals, accum)

    highest, totals, accum = lax.cond(jnp.any(key_mask), attend, lambda current: current, state)
    log_total = highest + jnp.log(totals)
    attn_heads = (accum / totals[..., None]).astype(jnp.bfloat16)
    attention_row_block = attn_heads.transpose(2, 0, 1, 3).reshape(row_count, query_columns)
    attn_out = jnp.einsum(
        "tc,jc->tj", attention_row_block, out_full, preferred_element_type=jnp.float32
    )
    residual = inputs + attn_out
    factor2, unit2 = unit_rows(residual)
    normed2 = (unit2 * norm2_gain).astype(jnp.bfloat16)
    gate_full, up_full, down_full = (
        lax.all_gather(w_gate, ("seq", "ctx"), axis=0, tiled=True),
        lax.all_gather(w_up, ("seq", "ctx"), axis=0, tiled=True),
        lax.all_gather(w_down, ("seq", "ctx"), axis=0, tiled=True),
    )
    gate = jnp.dot(normed2, gate_full, preferred_element_type=jnp.float32)
    upward = jnp.dot(normed2, up_full, preferred_element_type=jnp.float32)
    sigmoid = jax.nn.sigmoid(gate)
    activation = gate * sigmoid
    hidden_units = (activation * upward).astype(jnp.bfloat16)
    mlp_out = jnp.einsum("tf,jf->tj", hidden_units, down_full, preferred_element_type=jnp.float32)
    out_hidden = (residual + mlp_out).astype(jnp.bfloat16)
    grad_out_b = cotangent[0]
    grad_hidden = jnp.dot(grad_out_b, down_full, preferred_element_type=jnp.float32)
    grad_gate = (grad_hidden * upward * sigmoid * (1.0 + gate * (1.0 - sigmoid))).astype(
        jnp.bfloat16
    )
    grad_up = (grad_hidden * activation).astype(jnp.bfloat16)
    grad_normed2 = jnp.einsum(
        "tf,jf->tj", grad_gate, gate_full, preferred_element_type=jnp.float32
    ) + jnp.einsum("tf,jf->tj", grad_up, up_full, preferred_element_type=jnp.float32)
    gain2_local = jnp.sum(grad_normed2 * unit2, 0)
    grad_residual = grad_out_b.astype(jnp.float32) + unit_back(
        grad_normed2 * norm2_gain, factor2, unit2
    )
    grad_residual_b = grad_residual.astype(jnp.bfloat16)
    grad_attn = jnp.dot(grad_residual_b, out_full, preferred_element_type=jnp.float32)
    attention_gradient_backward = grad_attn.astype(jnp.bfloat16)
    head_gradient = attention_gradient_backward.reshape(
        row_count, kv_heads, query_group_count, head_width
    ).transpose(1, 2, 0, 3)
    delta_rows = jnp.sum(head_gradient.astype(jnp.float32) * attn_heads.astype(jnp.float32), -1)
    grads_full = jnp.zeros((2, row_count * cycle_size, kv_heads, head_width), jnp.float32)
    grad_q_acc = jnp.zeros((kv_heads, query_group_count, row_count, head_width), jnp.float32)
    current = (grads_full, grad_q_acc)
    backward_key_value_couple = lax.all_gather(own_pair, "ctx", axis=1, tiled=True)
    piece_rows = backward_key_value_couple.shape[1]
    backward_key_mask = visible(piece_rows)

    def attend_back(inner):
        scores = block_scores(backward_key_value_couple, backward_key_mask)
        probs = jnp.exp(scores - log_total[..., None])
        probability_backward = probs.astype(jnp.bfloat16)
        grad_probs = jnp.einsum(
            "ekla,xea->eklx",
            head_gradient,
            backward_key_value_couple[1],
            preferred_element_type=jnp.float32,
        )
        score_gradient = (probs * (grad_probs - delta_rows[..., None])).astype(jnp.bfloat16)
        grad_q_acc = score_scale * jnp.einsum(
            "emaj,jep->emap",
            score_gradient,
            backward_key_value_couple[0],
            preferred_element_type=jnp.float32,
        )
        grad_keys = score_scale * jnp.einsum(
            "kejx,kejy->xky", score_gradient, query_head_rows, preferred_element_type=jnp.float32
        )
        grad_values = jnp.einsum(
            "kejx,kejy->xky",
            probability_backward,
            head_gradient,
            preferred_element_type=jnp.float32,
        )
        grads_full = jnp.stack((grad_keys, grad_values))
        return (grads_full, grad_q_acc)

    grads_full, grad_q_acc = lax.cond(
        jnp.any(backward_key_mask), attend_back, lambda inner: inner, current
    )
    grads_kv = lax.psum_scatter(
        grads_full.astype(jnp.bfloat16), "ctx", scatter_dimension=1, tiled=True
    ).astype(jnp.float32)
    grad_query = rotate_back(
        grad_q_acc.transpose(2, 0, 1, 3).reshape(
            row_count, query_columns // head_width, head_width
        ),
        cosine,
        sine,
    )
    grad_key = rotate_back(grads_kv[0], cosine, sine)
    qgain_local = jnp.sum(grad_query * query_unit, (0, 1))
    kgain_local = jnp.sum(grad_key * key_unit, (0, 1))
    grad_query_raw = unit_back(grad_query * query_gain, query_factor, query_unit)
    grad_key_raw = unit_back(grad_key * key_gain, key_factor, key_unit)
    grad_joint = jnp.concatenate(
        (
            grad_query_raw.reshape(row_count, query_columns),
            grad_key_raw.reshape(row_count, key_value_columns),
            grads_kv[1].reshape(row_count, key_value_columns),
        ),
        1,
    ).astype(jnp.bfloat16)
    grad_normed1 = jnp.einsum(
        "tc,jc->tj", grad_joint, joint_full, preferred_element_type=jnp.float32
    )
    gain1_local = jnp.sum(grad_normed1 * unit1, 0)
    grad_inputs = (grad_residual + unit_back(grad_normed1 * norm1_gain, factor1, unit1)).astype(
        jnp.bfloat16
    )
    joined = lax.psum_scatter(
        jnp.concatenate(
            (
                jnp.concatenate(
                    (
                        outer_rows(normed1, grad_joint),
                        outer_rows(grad_residual_b, attention_row_block),
                    ),
                    1,
                ),
                jnp.concatenate(
                    (
                        outer_rows(normed2, grad_gate),
                        outer_rows(normed2, grad_up),
                        outer_rows(grad_out_b, hidden_units),
                    ),
                    1,
                ),
            ),
            1,
        ),
        ("seq", "ctx"),
        scatter_dimension=0,
        tiled=True,
    )
    attn_grads = joined[:, :attn_width]
    mlp_grads = joined[:, attn_width:]
    gain_totals = lax.psum((gain1_local, gain2_local, qgain_local, kgain_local), ("seq", "ctx"))
    hidden_width = w_gate.shape[1]
    return (
        out_hidden[None],
        grad_inputs[None],
        attn_grads[:, :query_columns],
        attn_grads[:, query_columns : query_columns + key_value_columns],
        attn_grads[:, query_columns + key_value_columns : query_columns + 2 * key_value_columns],
        attn_grads[:, query_columns + 2 * key_value_columns :],
        mlp_grads[:, :hidden_width],
        mlp_grads[:, hidden_width : 2 * hidden_width],
        mlp_grads[:, 2 * hidden_width :],
        gain_totals[0],
        gain_totals[1],
        gain_totals[2],
        gain_totals[3],
    )


def solution(mesh):
    placed = (
        P("seq", "ctx", None),
        P("seq", "ctx"),
        P(),
        P(("seq", "ctx"), None),
        P(("seq", "ctx"), None),
        P(("seq", "ctx"), None),
        P(),
        P(),
        P(("seq", "ctx"), None),
        P(),
        P(("seq", "ctx"), None),
        P(("seq", "ctx"), None),
        P(("seq", "ctx"), None),
        P("seq", "ctx", None),
    )
    return jax.shard_map(
        shards,
        mesh=mesh,
        in_specs=placed,
        out_specs=(
            P("seq", "ctx", None),
            P("seq", "ctx", None),
            P(("seq", "ctx"), None),
            P(("seq", "ctx"), None),
            P(("seq", "ctx"), None),
            P(("seq", "ctx"), None),
            P(("seq", "ctx"), None),
            P(("seq", "ctx"), None),
            P(("seq", "ctx"), None),
            P(),
            P(),
            P(),
            P(),
        ),
        check_vma=False,
    )
```

profile of v0, /device:TPU:0, one launch (start us, length us, event | category | flops | bytes accessed | tf_op | source)
XLA Modules:
  0.0 1033.1 jit_solution(10262787991396275115)
XLA Ops:
  7.2 1.7 pad_maximum_fusion.7
  9.0 1.1 fusion.58
  11.1 80.1 %all-gather.7.cloned.1.call-done = bf16[1024,4096]{1,0:T(8,128)(2,1)} async-done(((bf16[32,4096]{1,0:T(8,128)(2,1)}), bf16[1024,4096]{1,0:T(8,128)(2,1)}) %all-gather.7.cloned.1.call-update) | async-done | bytes 8388624 | tf_op jit(solution)/shard_map/all_gather | solution.py:81
  91.2 4.8 fusion.78
  97.2 1.0 pad_maximum_fusion.3
  100.8 1.4 fusion.73
  104.7 1.1 maximum_bitcast_fusion
  105.8 13.8 %all-gather.9.cloned.1.call-done = bf16[2,512,8,128]{3,1,2,0:T(8,128)(2,1)} async-done(((bf16[2,128,8,128]{3,1,2,0:T(8,128)(2,1)}), bf16[2,512,8,128]{3,1,2,0:T(8,128)(2,1)}) %all-gather.9.cloned.1.call-update) | async-done | bytes 2097168 | tf_op jit(solution)/shard_map/all_gather | solution.py:130
  119.6 11.9 %conditional.2 = (f32[8,2,128]{2,1,0:T(2,128)}, f32[8,2,128]{2,1,0:T(2,128)S(1)}, f32[8,2,128]{2,1,0:T(2,128)}, f32[8,2,128,128]{2,3,1,0:T(8,128)}) conditional(s32[]{:T(128)} %convert_element_type.93, () %tuple.26, (pred[128,512]{1,0:T(8,128)(4,1)}, bf16[2,512,8,128]{3,1,2,0:T(8,128)(2,1)}, bf16[8,2,128,128]{3,2,1,0:T(8,128)(2,1)}) %tuple.27), branch_computations={%region_4.0_spmd, %region_5.8_spmd} | conditional | flops 548669440 | bytes 27279448 | solution.py:148
  119.6 2.9 fusion
  122.5 1.7 fusion.2
  124.2 1.3 fusion.84
  125.6 2.9 fusion.9
  128.5 2.5 copy.136
  131.5 2.6 fusion.86
  134.1 50.1 %all-gather.11.cloned.1.call-done = bf16[1024,2048]{1,0:T(8,128)(2,1)} async-done(((bf16[32,2048]{1,0:T(8,128)(2,1)}), bf16[1024,2048]{1,0:T(8,128)(2,1)}) %all-gather.11.cloned.1.call-update) | async-done | bytes 4194320 | tf_op jit(solution)/shard_map/all_gather | solution.py:82
  184.2 3.9 multiply_reduce_fusion.6
  188.2 0.8 copy-done.2
  189.1 65.8 %all-gather.15.cloned.1.call-done = bf16[1024,3072]{1,0:T(8,128)(2,1)} async-done(((bf16[32,3072]{1,0:T(8,128)(2,1)}), bf16[1024,3072]{1,0:T(8,128)(2,1)}) %all-gather.15.cloned.1.call-update) | async-done | bytes 6291472 | tf_op jit(solution)/shard_map/all_gather | solution.py:160
  254.9 5.0 fusion.92
  259.8 65.5 %all-gather.13.cloned.1.call-done = bf16[1024,3072]{1,0:T(8,128)(2,1)} async-done(((bf16[32,3072]{1,0:T(8,128)(2,1)}), bf16[1024,3072]{1,0:T(8,128)(2,1)}) %all-gather.13.cloned.1.call-update) | async-done | bytes 6291472 | tf_op jit(solution)/shard_map/all_gather | solution.py:159
  325.3 4.9 fusion.91
  330.2 65.5 %all-gather.17.cloned.1.call-done = bf16[1024,3072]{1,0:T(8,128)(2,1)} async-done(((bf16[32,3072]{1,0:T(8,128)(2,1)}), bf16[1024,3072]{1,0:T(8,128)(2,1)}) %all-gather.17.cloned.1.call-update) | async-done | bytes 6291472 | tf_op jit(solution)/shard_map/all_gather | solution.py:161
  395.8 6.5 multiply_convert_fusion.1
  402.3 2.2 fusion.93
  404.6 5.9 multiply_reduce_fusion.3
  410.7 0.8 copy-done.5
  411.5 1.5 convolution_convert_fusion
  413.1 2.2 reshape.242
  415.3 2.4 fusion.83
  417.7 14.5 %conditional.3 = (bf16[2,512,8,128]{3,1,2,0:T(8,128)(2,1)}, f32[8,2,128,128]{3,2,1,0:T(8,128)}) conditional(s32[]{:T(128)} %convert_element_type.93, () %tuple.28, (pred[128,512]{1,0:T(8,128)(4,1)}, bf16[2,512,8,128]{3,1,2,0:T(8,128)(2,1)}, bf16[8,2,128,128]{3,2,1,0:T(8,128)(2,1)}, f32[8,2,128]{2,1,0:T(2,128)}, f32[8,2,128]{2,1,0:T(2,128)}, ...), branch_computations={%region_10.11_spmd, %region_11.0_spmd} | conditional | flops 1355546624 | bytes 48685184 | solution.py:226
  417.7 2.6 copy.118
  420.3 2.0 multiply_reduce_fusion
  422.9 2.1 fusion.33
  425.1 1.5 fusion.28
  426.7 1.4 multiply_convert_fusion
  428.1 1.7 convolution_multiply_fusion
  429.8 0.8 fusion.23
  430.6 1.5 pad_maximum_fusion
  433.6 0.7 copy.139
  434.3 1.9 fusion.90
  436.3 1.3 multiply_add_fusion
  437.6 1.0 multiply_reduce_fusion.1
  439.2 2.2 fusion.46
  441.4 20.6 %reduce-scatter.3.cloned.1.call-done = bf16[2,128,8,128]{3,1,2,0:T(8,128)(2,1)} async-done(((bf16[2,512,8,128]{3,1,2,0:T(8,128)(2,1)}), bf16[2,128,8,128]{3,1,2,0:T(8,128)(2,1)}) %reduce-scatter.3.cloned.1.call-update) | async-done | bytes 524304 | tf_op jit(solution)/shard_map/reduce_scatter | solution.py:229
  462.0 1.1 fusion.69
  463.3 0.8 copy.174
  464.4 1.8 fusion.74
  466.3 1.0 mul.412.clone
  467.5 1.4 fusion.62
  468.9 9.6 convolution_dynamic-update-slice_fusion
  478.5 4.6 convolution_dynamic-update-slice_fusion.3
  483.1 6.4 convolution_dynamic-update-slice_fusion.2
  489.5 6.6 convolution_dynamic-update-slice_fusion.1
  496.1 6.4 bitcast_dynamic-update-slice_fusion
  502.7 0.9 copy-done.4
  503.6 5.7 fusion.42
  509.3 6.8 fusion.57
  516.2 39.6 %all-reduce = (f32[1024]{0:T(1024)}, f32[1024]{0:T(1024)}, f32[128]{0:T(128)}, f32[128]{0:T(128)}) all-reduce(f32[1024]{0:T(1024)S(1)} %get-tuple-element.106, f32[1024]{0:T(1024)S(1)} %copy-done.37, f32[128]{0:T(128)S(1)} %bitcast_reduce_fusion, f32[128]{0:T(128)S(1)} %bitcast_reduce_fusion.1), channel_id=1, replica_groups=mesh['seq'=8,'ctx'=4] {'seq','ctx'}, use_global_device_ids=true, to_apply=%region_19.20 | all-reduce | flops 2304 | bytes 18432 | tf_op jit(solution)/shard_map/psum | solution.py:286
  555.8 0.9 fusion.68
  556.7 463.5 %reduce-scatter.5.cloned.1.call-done = f32[32,15360]{1,0:T(8,128)} async-done(((f32[1024,15360]{1,0:T(8,128)}), f32[32,15360]{1,0:T(8,128)}) %reduce-scatter.5.cloned.1.call-update) | async-done | bytes 1966096 | tf_op jit(solution)/shard_map/reduce_scatter | solution.py:259
  1020.2 1.7 fusion.89
  1021.9 1.9 fusion.88
  1023.7 2.3 fusion.87
  (140 shorter events, 10.6 us)
Async XLA Ops:
  7.2 84.0 %all-gather.7.cloned.1.call-start = ((), (), s32[]{:S(2)}) async-start(), calls=%async_computation.2 | async-start | bytes 8650752 | tf_op jit(solution)/shard_map/all_gather | solution.py:81
  8.9 110.6 %all-gather.9.cloned.1.call-start = ((), (), s32[]{:S(2)}) async-start(), calls=%async_computation.3 | async-start | bytes 2621440 | tf_op jit(solution)/shard_map/all_gather | solution.py:130
  10.8 80.5 %copy-start.35 = (f32[128]{0:T(128)}, f32[128]{0:T(128)S(1)}, u32[]{:S(2)}) copy-start(f32[128]{0:T(128)S(1)} %add_rsqrt_fusion.3) | copy-start | bytes 1540
  96.0 0.7 copy-start.40
  96.2 6.6 copy-start.11
  96.2 4.5 copy-start.42
  97.2 6.3 copy-start.38
  98.2 86.0 %all-gather.11.cloned.1.call-start = ((), (), s32[]{:S(2)}) async-start(), calls=%async_computation.4 | async-start | bytes 4325376 | tf_op jit(solution)/shard_map/all_gather | solution.py:82
  99.0 155.9 %all-gather.15.cloned.1.call-start = ((), (), s32[]{:S(2)}) async-start(), calls=%async_computation.6 | async-start | bytes 6488064 | tf_op jit(solution)/shard_map/all_gather | solution.py:160
  99.5 225.8 %all-gather.13.cloned.1.call-start = ((), (), s32[]{:S(2)}) async-start(), calls=%async_computation.5 | async-start | bytes 6488064 | tf_op jit(solution)/shard_map/all_gather | solution.py:159
  100.1 295.6 %all-gather.17.cloned.1.call-start = ((), (), s32[]{:S(2)}) async-start(), calls=%async_computation.7 | async-start | bytes 6488064 | tf_op jit(solution)/shard_map/all_gather | solution.py:161
  100.7 361.3 %reduce-scatter.3.cloned.1.call-start = ((), (), s32[]{:S(2)}) async-start(), calls=%async_computation.8 | async-start | bytes 2621440 | tf_op jit(solution)/shard_map/reduce_scatter | solution.py:229
  103.5 2.3 copy-start.27
  119.6 64.6 %copy-start.8 = (bf16[1,128,1024]{2,1,0:T(8,128)(2,1)S(1)}, bf16[1,128,1024]{2,1,0:T(8,128)(2,1)}, u32[]{:S(2)}) copy-start(bf16[1,128,1024]{2,1,0:T(8,128)(2,1)} %param.18) | copy-start | bytes 786436
  119.6 2.9 copy-start.29
  119.6 6.0 copy-start.20
  131.5 57.5 %copy-start.33 = (f32[1024]{0:T(1024)S(1)}, f32[1024]{0:T(1024)}, u32[]{:S(2)}) copy-start(f32[1024]{0:T(1024)} %param.27) | copy-start | bytes 12292
  188.1 0.8 copy-start.2
  395.8 6.6 copy-start
  402.3 8.2 copy-start.15
  402.3 8.2 copy-start.17
  402.3 2.2 copy-start.3
  404.5 6.0 copy-start.22
  404.6 7.0 copy-start.1
  410.7 0.8 copy-start.5
  417.7 14.7 %copy-start.41 = (f32[128]{0:T(128)S(1)}, f32[128]{0:T(128)}, u32[]{:S(2)}) copy-start(f32[128]{0:T(128)} %param.25) | copy-start | bytes 1540
  417.7 15.3 %copy-start.39 = (f32[128]{0:T(128)S(1)}, f32[128]{0:T(128)}, u32[]{:S(2)}) copy-start(f32[128]{0:T(128)} %param.24) | copy-start | bytes 1540
  420.3 4.8 copy-start.30
  420.3 4.8 copy-start.31
  425.1 1.6 copy-start.21
  428.1 1.7 copy-start.7
  432.2 588.0 %reduce-scatter.5.cloned.1.call-start = ((), (), s32[]{:S(2)}) async-start(), calls=%async_computation.9 | async-start | bytes 64880640 | tf_op jit(solution)/shard_map/reduce_scatter | solution.py:259
  434.3 3.2 copy-start.28
  437.5 1.7 copy-start.34
  439.2 25.1 %copy-start.12 = (f32[16,8,8,128]{3,2,1,0:T(8,128)S(1)}, f32[16,8,8,128]{3,2,1,0:T(8,128)}, u32[]{:S(2)}) copy-start(f32[16,8,8,128]{3,2,1,0:T(8,128)} %copy-done.11) | copy-start | bytes 1572868
  463.3 5.6 copy-start.9
  463.3 5.6 copy-start.32
  468.9 9.6 copy-start.24
  468.9 9.6 copy-start.6
  468.9 9.6 copy-start.13
  478.5 4.6 copy-start.16
  483.1 6.4 copy-start.18
  489.5 6.6 copy-start.14
  489.5 6.6 copy-start.23
  502.5 1.0 copy-start.4
  502.6 6.7 copy-start.10
  502.6 6.7 copy-start.19
  502.6 6.7 copy-start.25
  502.6 6.7 copy-start.26
  502.6 6.7 copy-start.36
  509.3 6.8 copy-start.37
Sparse Core Ops, SparseCore 0:
  11.4 79.7 all-gather.6
  98.3 21.1 all-gather.8
  122.4 61.7 all-gather.10
  186.9 67.9 all-gather.14
  257.6 67.6 all-gather.12
  328.0 67.6 all-gather.16
  432.3 29.6 reduce-scatter.2
  502.7 517.4 reduce-scatter.4
where the time goes:
time: 1040 us; the launch traced here: 1030 us
  waiting for transfers between devices  827 us (80%)
  matrix products  94.4 us (9%)
  blocking collectives  39.6 us (4%)
  other arithmetic  31.6 us (3%)
  local copies, waits for them, and re-layouts  23.6 us (2%)
  between operations  15.6 us (2%)
    reduce_scatter x1, waiting for transfers between devices, shards(): lax.psum_scatter(jnp.concatenate((jnp.concatenate((outer_rows(normed1, gr...  463 us
    all_gather x1, waiting for transfers between devices, shards(): lax.all_gather(w_joint, ('seq', 'ctx'), axis=0, tiled=True)  80.1 us
    all_gather x1, waiting for transfers between devices, shards(): lax.all_gather(w_up, ('seq', 'ctx'), axis=0, tiled=True)  65.8 us
    all_gather x1, waiting for transfers between devices, shards(): lax.all_gather(w_down, ('seq', 'ctx'), axis=0, tiled=True)  65.5 us
    all_gather x1, waiting for transfers between devices, shards(): lax.all_gather(w_gate, ('seq', 'ctx'), axis=0, tiled=True)  65.5 us
    all_gather x1, waiting for transfers between devices, shards(): lax.all_gather(w_out, ('seq', 'ctx'), axis=0, tiled=True)  50.1 us
    psum x1, blocking collectives, shards(): lax.psum((gain1_local, gain2_local, qgain_local, kgain_local), ('seq', 'c...  39.6 us
    dot_general x5, matrix products, outer_rows(): jnp.einsum('tj,tc->jc', left, right, preferred_element_type=jnp.float32)  33.6 us
  transfers between devices with their start and end apart: 8, of which 8 were waited for; matrix products, arithmetic and copies ran while one was open for 5% of the time, Pallas kernels for 0%

commit v1 on v0

--- a/solution.py
+++ b/solution.py
@@ -5,6 +5,11 @@
 
 NORM_EPSILON = 1e-06
 ROPE_THETA = 1000000.0
+
+
+def all_by_exchange(x, axis, dim):
+    outgoing = jnp.stack([x] * lax.axis_size(axis))
+    return jnp.concatenate(lax.all_to_all(outgoing, axis, 0, 0), axis=dim)
 
 
 def rope_tables(position_ids, head_width):
@@ -78,7 +83,7 @@
     normed1 = (unit1 * norm1_gain).astype(jnp.bfloat16)
     w_joint = jnp.concatenate((w_query, key_weight_matrix, value_weight_matrix), 1)
     joint_full, out_full = (
-        lax.all_gather(w_joint, ("seq", "ctx"), axis=0, tiled=True),
+        all_by_exchange(w_joint, ("seq", "ctx"), 0),
         lax.all_gather(w_out, ("seq", "ctx"), axis=0, tiled=True),
     )
     projected_output = jnp.dot(normed1, joint_full, preferred_element_type=jnp.float32)

time: 1040 us -> 1160 us (1.12)
  waiting for transfers between devices: 827 us -> 930 us
    all_to_all x0 -> x1, waiting for transfers between devices: none -> 185 us  [all_by_exchange(): return jnp.concatenate(lax.all_to_all(outgoing, axis, 0, 0), axis=dim)]
    all_gather x1 -> x0, waiting for transfers between devices: 80.1 us -> none  [shards(): lax.all_gather(w_joint, ('seq', 'ctx'), axis=0, tiled=True)]
where the time goes in v1:
time: 1160 us; the launch traced here: 1150 us
  waiting for transfers between devices  930 us (80%)
  matrix products  94.3 us (8%)
  blocking collectives  39.6 us (3%)
  other arithmetic  30.9 us (3%)
  local copies, waits for them, and re-layouts  29.3 us (3%)
  between operations  15.8 us (1%)
    reduce_scatter x1, waiting for transfers between devices, shards(): lax.psum_scatter(jnp.concatenate((jnp.concatenate((outer_rows(normed1, gr...  464 us
    all_to_all x1, waiting for transfers between devices, all_by_exchange(): return jnp.concatenate(lax.all_to_all(outgoing, axis, 0, 0), axis=dim)  185 us
    all_gather x1, waiting for transfers between devices, shards(): lax.all_gather(w_up, ('seq', 'ctx'), axis=0, tiled=True)  66 us
    all_gather x1, waiting for transfers between devices, shards(): lax.all_gather(w_down, ('seq', 'ctx'), axis=0, tiled=True)  65.5 us
    all_gather x1, waiting for transfers between devices, shards(): lax.all_gather(w_gate, ('seq', 'ctx'), axis=0, tiled=True)  65.5 us
    all_gather x1, waiting for transfers between devices, shards(): lax.all_gather(w_out, ('seq', 'ctx'), axis=0, tiled=True)  50.3 us
    psum x1, blocking collectives, shards(): lax.psum((gain1_local, gain2_local, qgain_local, kgain_local), ('seq', 'c...  39.6 us
    dot_general x5, matrix products, outer_rows(): jnp.einsum('tj,tc->jc', left, right, preferred_element_type=jnp.float32)  33.6 us
  transfers between devices with their start and end apart: 8, of which 8 were waited for; matrix products, arithmetic and copies ran while one was open for 5% of the time, Pallas kernels for 0%

profile of v1, /device:TPU:0, one launch (start us, length us, event | category | flops | bytes accessed | tf_op | source)
XLA Modules:
  0.0 1148.2 jit_solution(535081191361211641)
XLA Ops:
  7.2 1.0 pad_maximum_fusion.7
  8.2 4.3 stack.10
  12.5 7.5 all-to-all-start
  20.5 185.3 %all-to-all-done = bf16[32,32,4096]{2,1,0:T(8,128)(2,1)} async-done(((bf16[32,32,4096]{2,1,0:T(8,128)(2,1)}), bf16[32,32,4096]{2,1,0:T(8,128)(2,1)}, u32[]{:S(2)}, u32[]{:S(2)}) %all-to-all-start) | async-done | bytes 8388640 | tf_op jit(solution)/shard_map/all_to_all | solution.py:12
  205.9 4.7 fusion.73
  210.8 0.8 copy.113
  212.5 1.9 pad_maximum_fusion.3
  217.8 1.4 fusion.85
  222.4 1.1 maximum_bitcast_fusion
  223.4 10.8 all-gather.6.cloned.1.call-done
  234.2 11.6 %conditional.2 = (f32[8,2,128]{2,1,0:T(2,128)}, f32[8,2,128]{2,1,0:T(2,128)}, f32[8,2,128]{2,1,0:T(2,128)}, f32[8,2,128,128]{2,3,1,0:T(8,128)}) conditional(s32[]{:T(128)} %convert_element_type.101, () %tuple.26, (pred[128,512]{1,0:T(8,128)(4,1)}, bf16[2,512,8,128]{3,1,2,0:T(8,128)(2,1)}, bf16[8,2,128,128]{3,2,1,0:T(8,128)(2,1)}) %tuple.27), branch_computations={%region_4.0_spmd, %region_5.8_spmd} | conditional | flops 548669440 | bytes 27279448 | solution.py:153
  234.2 2.9 fusion
  237.2 1.7 fusion.2
  238.9 1.3 fusion.93
  240.2 2.9 fusion.9
  243.2 2.5 copy.136
  245.9 2.6 fusion.95
  248.5 50.3 %all-gather.8.cloned.1.call-done = bf16[1024,2048]{1,0:T(8,128)(2,1)} async-done(((bf16[32,2048]{1,0:T(8,128)(2,1)}), bf16[1024,2048]{1,0:T(8,128)(2,1)}) %all-gather.8.cloned.1.call-update) | async-done | bytes 4194320 | tf_op jit(solution)/shard_map/all_gather | solution.py:87
  298.9 3.9 multiply_reduce_fusion.6
  302.8 0.8 copy-done.2
  303.7 66.0 %all-gather.12.cloned.1.call-done = bf16[1024,3072]{1,0:T(8,128)(2,1)} async-done(((bf16[32,3072]{1,0:T(8,128)(2,1)}), bf16[1024,3072]{1,0:T(8,128)(2,1)}) %all-gather.12.cloned.1.call-update) | async-done | bytes 6291472 | tf_op jit(solution)/shard_map/all_gather | solution.py:165
  369.7 5.0 fusion.101
  374.7 65.5 %all-gather.10.cloned.1.call-done = bf16[1024,3072]{1,0:T(8,128)(2,1)} async-done(((bf16[32,3072]{1,0:T(8,128)(2,1)}), bf16[1024,3072]{1,0:T(8,128)(2,1)}) %all-gather.10.cloned.1.call-update) | async-done | bytes 6291472 | tf_op jit(solution)/shard_map/all_gather | solution.py:164
  440.1 4.9 fusion.100
  445.1 65.5 %all-gather.14.cloned.1.call-done = bf16[1024,3072]{1,0:T(8,128)(2,1)} async-done(((bf16[32,3072]{1,0:T(8,128)(2,1)}), bf16[1024,3072]{1,0:T(8,128)(2,1)}) %all-gather.14.cloned.1.call-update) | async-done | bytes 6291472 | tf_op jit(solution)/shard_map/all_gather | solution.py:166
  510.6 6.5 multiply_convert_fusion.1
  517.2 2.2 fusion.102
  519.4 5.9 multiply_reduce_fusion.3
  525.5 0.8 copy-done.5
  526.3 1.5 convolution_convert_fusion
  527.9 2.2 reshape.262
  530.1 2.4 fusion.92
  532.5 14.4 %conditional.3 = (bf16[2,512,8,128]{3,1,2,0:T(8,128)(2,1)}, f32[8,2,128,128]{3,2,1,0:T(8,128)}) conditional(s32[]{:T(128)} %convert_element_type.101, () %tuple.28, (pred[128,512]{1,0:T(8,128)(4,1)}, bf16[2,512,8,128]{3,1,2,0:T(8,128)(2,1)}, bf16[8,2,128,128]{3,2,1,0:T(8,128)(2,1)}, f32[8,2,128]{2,1,0:T(2,128)}, f32[8,2,128]{2,1,0:T(2,128)}, ...), branch_computations={%region_10.11_spmd, %region_11.0_spmd} | conditional | flops 1355546624 | bytes 48685184 | solution.py:231
  532.5 2.6 copy.118
  535.1 2.0 multiply_reduce_fusion
  537.8 2.1 fusion.33
  539.9 1.5 fusion.28
  541.5 1.4 multiply_convert_fusion
  542.9 1.7 convolution_multiply_fusion
  544.6 0.8 fusion.23
  545.4 1.5 pad_maximum_fusion
  549.2 1.9 fusion.99
  551.1 1.3 multiply_add_fusion
  552.4 1.0 multiply_reduce_fusion.1
  554.1 2.2 fusion.46
  556.2 20.6 %reduce-scatter.3.cloned.1.call-done = bf16[2,128,8,128]{3,1,2,0:T(8,128)(2,1)} async-done(((bf16[2,512,8,128]{3,1,2,0:T(8,128)(2,1)}), bf16[2,128,8,128]{3,1,2,0:T(8,128)(2,1)}) %reduce-scatter.3.cloned.1.call-update) | async-done | bytes 524304 | tf_op jit(solution)/shard_map/reduce_scatter | solution.py:234
  576.8 1.1 fusion.77
  579.2 1.8 fusion.86
  581.1 1.0 mul.422.clone
  582.3 1.4 fusion.66
  583.7 9.6 convolution_dynamic-update-slice_fusion
  593.3 4.6 convolution_dynamic-update-slice_fusion.3
  597.9 6.4 convolution_dynamic-update-slice_fusion.2
  604.3 6.7 convolution_dynamic-update-slice_fusion.1
  611.0 6.4 bitcast_dynamic-update-slice_fusion
  617.5 0.9 copy-done.4
  618.4 5.7 fusion.42
  624.2 6.8 fusion.59
  631.0 39.6 %all-reduce = (f32[1024]{0:T(1024)}, f32[1024]{0:T(1024)}, f32[128]{0:T(128)}, f32[128]{0:T(128)}) all-reduce(f32[1024]{0:T(1024)S(1)} %get-tuple-element.106, f32[1024]{0:T(1024)S(1)} %copy-done.37, f32[128]{0:T(128)S(1)} %bitcast_reduce_fusion, f32[128]{0:T(128)S(1)} %bitcast_reduce_fusion.1), channel_id=1, replica_groups=mesh['seq'=8,'ctx'=4] {'seq','ctx'}, use_global_device_ids=true, to_apply=%region_19.20 | all-reduce | flops 2304 | bytes 18432 | tf_op jit(solution)/shard_map/psum | solution.py:291
  670.6 0.9 fusion.76
  671.6 463.5 %reduce-scatter.5.cloned.1.call-done = f32[32,15360]{1,0:T(8,128)} async-done(((f32[1024,15360]{1,0:T(8,128)}), f32[32,15360]{1,0:T(8,128)}) %reduce-scatter.5.cloned.1.call-update) | async-done | bytes 1966096 | tf_op jit(solution)/shard_map/reduce_scatter | solution.py:264
  1135.1 1.7 fusion.98
  1136.8 1.9 fusion.97
  1138.6 2.3 fusion.96
  (142 shorter events, 13.0 us)
Async XLA Ops:
  12.5 7.5 copy-start.8
  12.5 7.7 copy-start.43
  12.5 193.4 %copy-start.32 = (f32[1024]{0:T(1024)S(1)}, f32[1024]{0:T(1024)}, u32[]{:S(2)}) copy-start(f32[1024]{0:T(1024)} %param.20) | copy-start | bytes 12292
  12.5 193.4 %all-to-all-start = ((bf16[32,32,4096]{2,1,0:T(8,128)(2,1)}), bf16[32,32,4096]{2,1,0:T(8,128)(2,1)}, u32[]{:S(2)}, u32[]{:S(2)}) async-start(bf16[32,32,4096]{2,1,0:T(8,128)(2,1)} %stack.10), calls=%async_computation | async-start | bytes 16777216 | tf_op jit(solution)/shard_map/all_to_all | solution.py:12
  20.0 214.3 %all-gather.6.cloned.1.call-start = ((), (), s32[]{:S(2)}) async-start(), calls=%async_computation.3 | async-start | bytes 2621440 | tf_op jit(solution)/shard_map/all_gather | solution.py:135
  20.2 190.4 %copy-start.35 = (f32[128]{0:T(128)}, f32[128]{0:T(128)S(1)}, u32[]{:S(2)}) copy-start(f32[128]{0:T(128)S(1)} %add_rsqrt_fusion.3) | copy-start | bytes 1540
  210.6 1.5 copy-start.39
  210.8 9.1 copy-start.11
  212.5 8.7 copy-start.38
  214.5 84.4 %all-gather.8.cloned.1.call-start = ((), (), s32[]{:S(2)}) async-start(), calls=%async_computation.4 | async-start | bytes 4325376 | tf_op jit(solution)/shard_map/all_gather | solution.py:87
  215.2 154.5 %all-gather.12.cloned.1.call-start = ((), (), s32[]{:S(2)}) async-start(), calls=%async_computation.6 | async-start | bytes 6488064 | tf_op jit(solution)/shard_map/all_gather | solution.py:165
  216.0 224.2 %all-gather.10.cloned.1.call-start = ((), (), s32[]{:S(2)}) async-start(), calls=%async_computation.5 | async-start | bytes 6488064 | tf_op jit(solution)/shard_map/all_gather | solution.py:164
  216.5 294.0 %all-gather.14.cloned.1.call-start = ((), (), s32[]{:S(2)}) async-start(), calls=%async_computation.7 | async-start | bytes 6488064 | tf_op jit(solution)/shard_map/all_gather | solution.py:166
  217.1 359.7 %reduce-scatter.3.cloned.1.call-start = ((), (), s32[]{:S(2)}) async-start(), calls=%async_computation.8 | async-start | bytes 2621440 | tf_op jit(solution)/shard_map/reduce_scatter | solution.py:234
  220.5 0.6 copy-start.27
  234.2 2.9 copy-start.29
  234.2 6.0 copy-start.20
  245.9 57.7 %copy-start.33 = (f32[1024]{0:T(1024)S(1)}, f32[1024]{0:T(1024)}, u32[]{:S(2)}) copy-start(f32[1024]{0:T(1024)} %param.27) | copy-start | bytes 12292
  302.8 0.8 copy-start.2
  302.8 0.8 copy-start.41
  510.6 6.6 copy-start
  517.1 8.2 copy-start.15
  517.1 8.2 copy-start.17
  517.1 2.2 copy-start.3
  517.1 2.2 copy-start.42
  519.4 5.9 copy-start.22
  519.4 7.0 copy-start.1
  525.5 0.8 copy-start.5
  532.5 14.7 %copy-start.40 = (f32[128]{0:T(128)S(1)}, f32[128]{0:T(128)}, u32[]{:S(2)}) copy-start(f32[128]{0:T(128)} %param.25) | copy-start | bytes 1540
  535.1 4.8 copy-start.30
  535.1 4.8 copy-start.31
  539.9 1.6 copy-start.21
  542.9 1.7 copy-start.7
  547.0 588.1 %reduce-scatter.5.cloned.1.call-start = ((), (), s32[]{:S(2)}) async-start(), calls=%async_computation.9 | async-start | bytes 64880640 | tf_op jit(solution)/shard_map/reduce_scatter | solution.py:264
  549.2 3.2 copy-start.28
  552.4 1.7 copy-start.34
  554.1 25.1 %copy-start.12 = (f32[16,8,8,128]{3,2,1,0:T(8,128)S(1)}, f32[16,8,8,128]{3,2,1,0:T(8,128)}, u32[]{:S(2)}) copy-start(f32[16,8,8,128]{3,2,1,0:T(8,128)} %copy-done.11) | copy-start | bytes 1572868
  578.1 5.6 copy-start.9
  583.7 9.6 copy-start.24
  583.7 9.6 copy-start.6
  583.7 9.6 copy-start.13
  593.3 4.6 copy-start.16
  597.9 6.4 copy-start.18
  604.3 6.7 copy-start.14
  604.3 6.7 copy-start.23
  617.4 1.0 copy-start.4
  617.4 6.7 copy-start.10
  617.4 6.7 copy-start.19
  617.4 6.7 copy-start.25
  617.4 6.7 copy-start.26
  617.5 6.7 copy-start.36
  624.2 6.9 copy-start.37
Sparse Core Ops, SparseCore 0:
  214.6 19.5 all-gather.5
  237.1 61.7 all-gather.7
  301.7 67.9 all-gather.11
  372.4 67.6 all-gather.9
  442.9 67.6 all-gather.13
  547.1 29.6 reduce-scatter.2
  617.5 517.5 reduce-scatter.4
